TPU v7x, 32 devices: a whole 2x2x4 slice. The times are simulated.
32 devices in a mesh: row: 8 (over y, x, core), col: 4 (over z).
Axes of the slice: x: 2, y: 2, z: 4, core: 2. Of those that a mesh axis runs over, the one named last changes fastest.
Arguments:
- contact_map: bfloat16 [512, 512, 128], P('row', 'col'), may hold values from -6 to 6
- conv_weight: bfloat16 [2, 3, 3, 3, 128, 128], replicated, may hold values from -0.1875 to 0.1875
- conv_bias: float32 [2, 3, 128], replicated, may hold values from -0.5 to 0.5
Outputs:
- trunk_out: bfloat16 [512, 512, 128], P('row', 'col')
All inputs are finite; a program needn't handle non-finite values.
Results may differ from a plain program's by a relative error of at most 0.0085.
Values may be sent and summed in bfloat16 or wider, within the bound.
A program may use at most 128 MiB of HBM per device.

v0:
```python
import jax
import jax.numpy as jnp
from jax import lax
from jax.sharding import PartitionSpec as P


def with_halo(array, sides, width):
    for axis, dim in sides:
        devices, length = (lax.axis_size(axis), array.shape[dim])
        up = [(i, (i + 1) % devices) for i in range(devices - 1)]
        down = [(j, i) for i, j in up]
        last = lax.slice_in_dim(array, length - width, length, axis=dim)
        initial = lax.slice_in_dim(array, 0, width, axis=dim)
        before = lax.ppermute(last, axis, up)
        after = lax.ppermute(initial, axis, down)
        array = jnp.concatenate([before, array, after], axis=dim)
    return array


def convolve(padded, kernel, rows, cols, dilation):
    total = jnp.zeros((rows, cols, kernel.shape[3]), jnp.float32)
    for tap_row in range(3):
        for tap_col in range(3):
            piece = padded[
                tap_row * dilation : tap_row * dilation + rows,
                tap_col * dilation : tap_col * dilation + cols,
            ]
            total = total + jnp.dot(
                piece, kernel[tap_row, tap_col], preferred_element_type=jnp.float32
            )
    return total


def average(current, flipped):
    return ((current.astype(jnp.float32) + flipped.astype(jnp.float32)) * 0.5).astype(jnp.bfloat16)


def strip_pad(hidden, dilation):
    widened = jnp.pad(hidden, ((0, 0), (dilation, dilation), (0, 0)))
    return with_halo(widened, ((("row", "col"), 0),), dilation)


def run_block(current, flipped, conv_weight, conv_bias, block, padder):
    rows, cols = (current.shape[0], current.shape[1])
    mirrored = average(current, flipped)
    hidden = mirrored
    result = mirrored
    for layer, dilation in enumerate((1, 2, 4)):
        padded = padder(hidden, dilation)
        total = (
            convolve(padded, conv_weight[block, layer], rows, cols, dilation)
            + conv_bias[block, layer]
        )
        if layer < 2:
            hidden = jax.nn.relu(total).astype(jnp.bfloat16)
        else:
            result = (mirrored.astype(jnp.float32) + total).astype(jnp.bfloat16)
    return result


def per_device(contact_map, conv_weight, conv_bias):
    blocks = conv_weight.shape[0]
    current = lax.all_to_all(contact_map, "col", split_axis=0, concat_axis=1, tiled=True)
    for block in range(blocks):
        columns = lax.all_to_all(current, ("row", "col"), split_axis=1, concat_axis=0, tiled=True)
        flipped = jnp.transpose(columns, (1, 0, 2))
        current = run_block(current, flipped, conv_weight, conv_bias, block, strip_pad)
    return lax.all_to_all(current, "col", split_axis=1, concat_axis=0, tiled=True)


def solution(mesh):
    in_specs = (P("row", "col", None), P(), P())
    out_specs = P("row", "col", None)
    return jax.shard_map(
        per_device, mesh=mesh, in_specs=in_specs, out_specs=out_specs, check_vma=False
    )
```

profile of v0, /device:TPU:0, one launch (start us, length us, event | category | flops | bytes accessed | tf_op | source)
XLA Modules:
  0.0 503.3 jit_solution(15225654004325715221)
XLA Ops:
  0.0 54.5 %all_to_all.54 = bf16[64,128,128]{2,1,0:T(8,128)(2,1)S(1)} all-to-all(bf16[64,128,128]{2,1,0:T(8,128)(2,1)} %param.3), channel_id=1, replica_groups=mesh['row'=8,'col'=4] {'col'}, dimensions={0} | all-to-all | bytes 4194304 | tf_op jit(solution)/shard_map/all_to_all | solution.py:63
  57.3 4.0 all-to-all-start.1
  64.2 44.6 %all-to-all-done.1 = bf16[16,512,128]{2,0,1:T(8,128)(2,1)} async-done(((bf16[16,512,128]{2,0,1:T(8,128)(2,1)}), bf16[16,512,128]{2,0,1:T(8,128)(2,1)}, u32[]{:S(2)}, u32[]{:S(2)}) %all-to-all-start.1) | async-done | bytes 2097184 | tf_op jit(solution)/shard_map/all_to_all | solution.py:65
  121.9 6.2 %collective-permute-start = (bf16[1,514,128]{2,1,0:T(8,128)(2,1)S(1)}, bf16[1,514,128]{2,1,0:T(8,128)(2,1)S(1)}, u32[]{:S(2)}, u32[]{:S(2)}) collective-permute-start(bf16[1,514,128]{2,1,0:T(8,128)(2,1)S(1)} %get-tuple-element.7), channel_id=1, source_target_pairs={{0,1},{1,2},{2,3},{3,4},{4,5},{5,6},{6,7},{7,8},{8,9},{9,10},{10,1... | collective-permute-start | bytes 394760 | tf_op jit(solution)/shard_map/ppermute | solution.py:14
  139.3 2.7 fusion.104
  142.1 11.9 %maximum_convert_fusion.3 = bf16[16,512,128]{2,1,0:T(8,128)(2,1)S(1)} fusion(f32[16,512,128]{2,1,0:T(8,128)} %fusion.65, f32[16,512,128]{2,1,0:T(8,128)} %fusion.68, f32[16,512,128]{2,1,0:T(8,128)} %fusion.128, f32[16,512,128]{2,1,0:T(8,128)} %fusion.145, f32[16,512,128]{2,1,0:T(8,128)} %fusion.130, f32[16,512,128]{2,1,0:T(8,128)} %fusion.104, ...), kind=kOutput, calls=%fused_computation.11 | convolution fusion | flops 284164096 | bytes 37947904 | tf_op jit(solution)/shard_map/dot_general | solution.py:28
  160.4 3.9 collective-permute-start.2
  168.5 10.3 %collective-permute-done.3 = bf16[2,516,128]{2,1,0:T(8,128)(2,1)S(1)} collective-permute-done((bf16[2,516,128]{2,1,0:T(8,128)(2,1)S(1)}, bf16[2,516,128]{2,1,0:T(8,128)(2,1)S(1)}, u32[]{:S(2)}, u32[]{:S(2)}) %collective-permute-start.3) | collective-permute-done | bytes 264224 | tf_op jit(solution)/shard_map/ppermute | solution.py:15
  189.5 2.7 fusion.98
  192.2 11.9 %maximum_convert_fusion.2 = bf16[16,512,128]{2,1,0:T(8,128)(2,1)S(1)} fusion(f32[16,512,128]{2,1,0:T(8,128)} %fusion.17, f32[16,512,128]{2,1,0:T(8,128)} %fusion.20, f32[16,512,128]{2,1,0:T(8,128)} %fusion.124, f32[16,512,128]{2,1,0:T(8,128)} %fusion.144, f32[16,512,128]{2,1,0:T(8,128)} %fusion.126, f32[16,512,128]{2,1,0:T(8,128)} %fusion.98, ...), kind=kOutput, calls=%fused_computation.10 | convolution fusion | flops 284164096 | bytes 38081024 | tf_op jit(solution)/shard_map/dot_general | solution.py:28
  211.6 4.8 collective-permute-start.4
  235.4 11.8 %add_convert_fusion.1 = bf16[16,512,128]{2,1,0:T(8,128)(2,1)S(1)} fusion(f32[16,512,128]{2,1,0:T(8,128)} %fusion.41, f32[16,512,128]{2,1,0:T(8,128)} %fusion.44, f32[16,512,128]{2,1,0:T(8,128)} %fusion.120, f32[16,512,128]{2,1,0:T(8,128)} %fusion.143, f32[16,512,128]{2,1,0:T(8,128)} %fusion.122, f32[16,512,128]{2,1,0:T(8,128)} %fusion.94, ...), kind=kOutput, calls=%fused_computation.9 | convolution fusion | flops 285212672 | bytes 40444416 | tf_op jit(solution)/shard_map/dot_general | solution.py:28
  248.6 59.4 %all_to_all.55 = bf16[16,512,128]{2,0,1:T(8,128)(2,1)S(1)} all-to-all(bf16[16,512,128]{2,0,1:T(8,128)(2,1)S(1)} %copy.11), channel_id=1, replica_groups=mesh['row'=8,'col'=4] {'row','col'}, dimensions={1} | all-to-all | bytes 4194304 | tf_op jit(solution)/shard_map/all_to_all | solution.py:65
  319.0 6.0 %collective-permute-start.6 = (bf16[1,514,128]{2,1,0:T(8,128)(2,1)S(1)}, bf16[1,514,128]{2,1,0:T(8,128)(2,1)S(1)}, u32[]{:S(2)}, u32[]{:S(2)}) collective-permute-start(bf16[1,514,128]{2,1,0:T(8,128)(2,1)S(1)} %get-tuple-element.5), channel_id=1, source_target_pairs={{0,1},{1,2},{2,3},{3,4},{4,5},{5,6},{6,7},{7,8},{8,9},{9,10},{10,1... | collective-permute-start | bytes 394760 | tf_op jit(solution)/shard_map/ppermute | solution.py:14
  335.7 2.7 fusion.88
  338.4 11.9 %maximum_convert_fusion.1 = bf16[16,512,128]{2,1,0:T(8,128)(2,1)S(1)} fusion(f32[16,512,128]{2,1,0:T(8,128)} %fusion.53, f32[16,512,128]{2,1,0:T(8,128)} %fusion.56, f32[16,512,128]{2,1,0:T(8,128)} %fusion.116, f32[16,512,128]{2,1,0:T(8,128)} %fusion.142, f32[16,512,128]{2,1,0:T(8,128)} %fusion.118, f32[16,512,128]{2,1,0:T(8,128)} %fusion.88, ...), kind=kOutput, calls=%fused_computation.8 | convolution fusion | flops 284164096 | bytes 37947904 | tf_op jit(solution)/shard_map/dot_general | solution.py:28
  356.4 3.9 collective-permute-start.8
  364.3 11.2 %collective-permute-done.9 = bf16[2,516,128]{2,1,0:T(8,128)(2,1)S(1)} collective-permute-done((bf16[2,516,128]{2,1,0:T(8,128)(2,1)S(1)}, bf16[2,516,128]{2,1,0:T(8,128)(2,1)S(1)}, u32[]{:S(2)}, u32[]{:S(2)}) %collective-permute-start.9) | collective-permute-done | bytes 264224 | tf_op jit(solution)/shard_map/ppermute | solution.py:15
  378.2 2.7 fusion.8
  386.2 2.7 fusion.82
  389.0 11.9 %maximum_convert_fusion = bf16[16,512,128]{2,1,0:T(8,128)(2,1)S(1)} fusion(f32[16,512,128]{2,1,0:T(8,128)} %fusion.5, f32[16,512,128]{2,1,0:T(8,128)} %fusion.8, f32[16,512,128]{2,1,0:T(8,128)} %fusion.112, f32[16,512,128]{2,1,0:T(8,128)} %fusion.141, f32[16,512,128]{2,1,0:T(8,128)} %fusion.114, f32[16,512,128]{2,1,0:T(8,128)} %fusion.82, ...), kind=kOutput, calls=%fused_computation.7 | convolution fusion | flops 284164096 | bytes 38081024 | tf_op jit(solution)/shard_map/dot_general | solution.py:28
  408.6 4.6 collective-permute-start.10
  431.9 11.8 %add_convert_fusion = bf16[16,512,128]{2,1,0:T(8,128)(2,1)S(1)} fusion(f32[16,512,128]{2,1,0:T(8,128)} %fusion.29, f32[16,512,128]{2,1,0:T(8,128)} %fusion.32, f32[16,512,128]{2,1,0:T(8,128)} %fusion.108, f32[16,512,128]{2,1,0:T(8,128)} %fusion.140, f32[16,512,128]{2,1,0:T(8,128)} %fusion.110, f32[16,512,128]{2,1,0:T(8,128)} %fusion.78, ...), kind=kOutput, calls=%fused_computation.6 | convolution fusion | flops 285212672 | bytes 40444416 | tf_op jit(solution)/shard_map/dot_general | solution.py:28
  445.0 56.2 %all_to_all.56 = bf16[16,512,128]{2,0,1:T(8,128)(2,1)S(1)} all-to-all(bf16[16,512,128]{2,0,1:T(8,128)(2,1)S(1)} %copy.13), channel_id=1, replica_groups=mesh['row'=8,'col'=4] {'col'}, dimensions={1} | all-to-all | bytes 4194304 | tf_op jit(solution)/shard_map/all_to_all | solution.py:68
  (90 shorter events, 148.3 us)
Async XLA Ops:
  57.3 4.0 copy-start.2
  57.3 51.5 %all-to-all-start.1 = ((bf16[16,512,128]{2,0,1:T(8,128)(2,1)}), bf16[16,512,128]{2,0,1:T(8,128)(2,1)}, u32[]{:S(2)}, u32[]{:S(2)}) async-start(bf16[16,512,128]{2,0,1:T(8,128)(2,1)} %copy.9), calls=%async_computation.1 | async-start | bytes 4194304 | tf_op jit(solution)/shard_map/all_to_all | solution.py:65
  111.7 1.0 copy-start.1
  117.9 10.7 %collective-permute-start.1 = (bf16[1,514,128]{2,1,0:T(8,128)(2,1)S(1)}, bf16[1,514,128]{2,1,0:T(8,128)(2,1)S(1)}, u32[]{:S(2)}, u32[]{:S(2)}) collective-permute-start(bf16[1,514,128]{2,1,0:T(8,128)(2,1)S(1)} %get-tuple-element.8), channel_id=1, source_target_pairs={{1,0},{2,1},{3,2},{4,3},{5,4},{6,5},{7,6},{8,7},{9,8},{10,9},{11,1... | collective-permute-start | bytes 394760 | tf_op jit(solution)/shard_map/ppermute | solution.py:15
  121.9 12.1 %collective-permute-start = (bf16[1,514,128]{2,1,0:T(8,128)(2,1)S(1)}, bf16[1,514,128]{2,1,0:T(8,128)(2,1)S(1)}, u32[]{:S(2)}, u32[]{:S(2)}) collective-permute-start(bf16[1,514,128]{2,1,0:T(8,128)(2,1)S(1)} %get-tuple-element.7), channel_id=1, source_target_pairs={{0,1},{1,2},{2,3},{3,4},{4,5},{5,6},{6,7},{7,8},{8,9},{9,10},{10,1... | collective-permute-start | bytes 394760 | tf_op jit(solution)/shard_map/ppermute | solution.py:14
  154.1 1.0 copy-start
  160.4 23.8 %collective-permute-start.2 = (bf16[2,516,128]{2,1,0:T(8,128)(2,1)S(1)}, bf16[2,516,128]{2,1,0:T(8,128)(2,1)S(1)}, u32[]{:S(2)}, u32[]{:S(2)}) collective-permute-start(bf16[2,516,128]{2,1,0:T(8,128)(2,1)S(1)} %get-tuple-element.15), channel_id=1, source_target_pairs={{0,1},{1,2},{2,3},{3,4},{4,5},{5,6},{6,7},{7,8},{8,9},{9,10},{10,1... | collective-permute-start | bytes 792584 | tf_op jit(solution)/shard_map/ppermute | solution.py:14
  164.3 14.5 %collective-permute-start.3 = (bf16[2,516,128]{2,1,0:T(8,128)(2,1)S(1)}, bf16[2,516,128]{2,1,0:T(8,128)(2,1)S(1)}, u32[]{:S(2)}, u32[]{:S(2)}) collective-permute-start(bf16[2,516,128]{2,1,0:T(8,128)(2,1)S(1)} %get-tuple-element.16), channel_id=1, source_target_pairs={{1,0},{2,1},{3,2},{4,3},{5,4},{6,5},{7,6},{8,7},{9,8},{10,9},{11,1... | collective-permute-start | bytes 792584 | tf_op jit(solution)/shard_map/ppermute | solution.py:15
  204.4 16.0 %collective-permute-start.5 = (bf16[4,520,128]{2,1,0:T(8,128)(2,1)S(1)}, bf16[4,520,128]{2,1,0:T(8,128)(2,1)S(1)}, u32[]{:S(2)}, u32[]{:S(2)}) collective-permute-start(bf16[4,520,128]{2,1,0:T(8,128)(2,1)S(1)} %get-tuple-element.14), channel_id=1, source_target_pairs={{1,0},{2,1},{3,2},{4,3},{5,4},{6,5},{7,6},{8,7},{9,8},{10,9},{11,1... | collective-permute-start | bytes 1597448 | tf_op jit(solution)/shard_map/ppermute | solution.py:15
  211.6 15.7 %collective-permute-start.4 = (bf16[4,520,128]{2,1,0:T(8,128)(2,1)S(1)}, bf16[4,520,128]{2,1,0:T(8,128)(2,1)S(1)}, u32[]{:S(2)}, u32[]{:S(2)}) collective-permute-start(bf16[4,520,128]{2,1,0:T(8,128)(2,1)S(1)} %get-tuple-element.13), channel_id=1, source_target_pairs={{0,1},{1,2},{2,3},{3,4},{4,5},{5,6},{6,7},{7,8},{8,9},{9,10},{10,1... | collective-permute-start | bytes 1597448 | tf_op jit(solution)/shard_map/ppermute | solution.py:14
  314.4 10.6 %collective-permute-start.7 = (bf16[1,514,128]{2,1,0:T(8,128)(2,1)S(1)}, bf16[1,514,128]{2,1,0:T(8,128)(2,1)S(1)}, u32[]{:S(2)}, u32[]{:S(2)}) collective-permute-start(bf16[1,514,128]{2,1,0:T(8,128)(2,1)S(1)} %get-tuple-element.6), channel_id=1, source_target_pairs={{1,0},{2,1},{3,2},{4,3},{5,4},{6,5},{7,6},{8,7},{9,8},{10,9},{11,1... | collective-permute-start | bytes 394760 | tf_op jit(solution)/shard_map/ppermute | solution.py:15
  319.0 11.4 %collective-permute-start.6 = (bf16[1,514,128]{2,1,0:T(8,128)(2,1)S(1)}, bf16[1,514,128]{2,1,0:T(8,128)(2,1)S(1)}, u32[]{:S(2)}, u32[]{:S(2)}) collective-permute-start(bf16[1,514,128]{2,1,0:T(8,128)(2,1)S(1)} %get-tuple-element.5), channel_id=1, source_target_pairs={{0,1},{1,2},{2,3},{3,4},{4,5},{5,6},{6,7},{7,8},{8,9},{9,10},{10,1... | collective-permute-start | bytes 394760 | tf_op jit(solution)/shard_map/ppermute | solution.py:14
  356.4 24.5 %collective-permute-start.8 = (bf16[2,516,128]{2,1,0:T(8,128)(2,1)S(1)}, bf16[2,516,128]{2,1,0:T(8,128)(2,1)S(1)}, u32[]{:S(2)}, u32[]{:S(2)}) collective-permute-start(bf16[2,516,128]{2,1,0:T(8,128)(2,1)S(1)} %get-tuple-element.11), channel_id=1, source_target_pairs={{0,1},{1,2},{2,3},{3,4},{4,5},{5,6},{6,7},{7,8},{8,9},{9,10},{10,1... | collective-permute-start | bytes 792584 | tf_op jit(solution)/shard_map/ppermute | solution.py:14
  360.3 15.2 %collective-permute-start.9 = (bf16[2,516,128]{2,1,0:T(8,128)(2,1)S(1)}, bf16[2,516,128]{2,1,0:T(8,128)(2,1)S(1)}, u32[]{:S(2)}, u32[]{:S(2)}) collective-permute-start(bf16[2,516,128]{2,1,0:T(8,128)(2,1)S(1)} %get-tuple-element.12), channel_id=1, source_target_pairs={{1,0},{2,1},{3,2},{4,3},{5,4},{6,5},{7,6},{8,7},{9,8},{10,9},{11,1... | collective-permute-start | bytes 792584 | tf_op jit(solution)/shard_map/ppermute | solution.py:15
  401.2 15.5 %collective-permute-start.11 = (bf16[4,520,128]{2,1,0:T(8,128)(2,1)S(1)}, bf16[4,520,128]{2,1,0:T(8,128)(2,1)S(1)}, u32[]{:S(2)}, u32[]{:S(2)}) collective-permute-start(bf16[4,520,128]{2,1,0:T(8,128)(2,1)S(1)} %get-tuple-element.10), channel_id=1, source_target_pairs={{1,0},{2,1},{3,2},{4,3},{5,4},{6,5},{7,6},{8,7},{9,8},{10,9},{11,1... | collective-permute-start | bytes 1597448 | tf_op jit(solution)/shard_map/ppermute | solution.py:15
  408.6 15.3 %collective-permute-start.10 = (bf16[4,520,128]{2,1,0:T(8,128)(2,1)S(1)}, bf16[4,520,128]{2,1,0:T(8,128)(2,1)S(1)}, u32[]{:S(2)}, u32[]{:S(2)}) collective-permute-start(bf16[4,520,128]{2,1,0:T(8,128)(2,1)S(1)} %get-tuple-element.9), channel_id=1, source_target_pairs={{0,1},{1,2},{2,3},{3,4},{4,5},{5,6},{6,7},{7,8},{8,9},{9,10},{10,1... | collective-permute-start | bytes 1597448 | tf_op jit(solution)/shard_map/ppermute | solution.py:14
  429.2 2.7 copy-start.3
where the time goes:
time: 508 us; the launch traced here: 503 us
  matrix products  200 us (39%)
  blocking collectives  170 us (33%)
  waiting for transfers between devices  71.7 us (14%)
  starting transfers between devices  41.4 us (8%)
  local copies, waits for them, and re-layouts  18.3 us (4%)
    dot_general x54, matrix products, convolve(): jnp.dot(piece, kernel[tap_row, tap_col], preferred_element_type=jnp.float32)  200 us
    all_to_all x1, blocking collectives, per_device(): lax.all_to_all(current, ('row', 'col'), split_axis=1, concat_axis=0, tile...  59.4 us
    all_to_all x1, blocking collectives, per_device(): lax.all_to_all(current, 'col', split_axis=1, concat_axis=0, tiled=True)  56.2 us
    all_to_all x1, blocking collectives, per_device(): lax.all_to_all(contact_map, 'col', split_axis=0, concat_axis=1, tiled=True)  54.5 us
    all_to_all x1, waiting for transfers between devices, per_device(): lax.all_to_all(current, ('row', 'col'), split_axis=1, concat_axis=0, tile...  44.6 us
    ppermute x6, starting transfers between devices, with_halo(): before = lax.ppermute(last, axis, up)  29.4 us
    ppermute x6, waiting for transfers between devices, with_halo(): after = lax.ppermute(initial, axis, down)  23.8 us
  transfers between devices with their start and end apart: 13, of which 7 were waited for; matrix products, arithmetic and copies ran while one was open for 13% of the time, Pallas kernels for 0%

commit v1 on v0

--- a/solution.py
+++ b/solution.py
@@ -2,6 +2,18 @@
 import jax.numpy as jnp
 from jax import lax
 from jax.sharding import PartitionSpec as P
+
+
+def rotated_exchange(x, axis, split, join):
+    ways, here = (lax.axis_size(axis), lax.axis_index(axis))
+    width = x.shape[split] // ways
+    turned = jnp.roll(x, -here * width, axis=split)
+    got = [lax.slice_in_dim(turned, 0, width, axis=split)]
+    for far in range(1, ways):
+        sent = lax.slice_in_dim(turned, far * width, (far + 1) * width, axis=split)
+        got.append(lax.ppermute(sent, axis, [(d, (d + far) % ways) for d in range(ways)]))
+    line = jnp.concatenate(got[::-1], axis=join)
+    return jnp.roll(line, (here + 1) * got[0].shape[join], axis=join)
 
 
 def with_halo(array, sides, width):
@@ -60,7 +72,7 @@
 
 def per_device(contact_map, conv_weight, conv_bias):
     blocks = conv_weight.shape[0]
-    current = lax.all_to_all(contact_map, "col", split_axis=0, concat_axis=1, tiled=True)
+    current = rotated_exchange(contact_map, "col", 0, 1)
     for block in range(blocks):
         columns = lax.all_to_all(current, ("row", "col"), split_axis=1, concat_axis=0, tiled=True)
         flipped = jnp.transpose(columns, (1, 0, 2))

time: 508 us -> 514 us (1.012)
  blocking collectives: 170 us -> 116 us
  waiting for transfers between devices: 71.7 us -> 115 us
  starting transfers between devices: 41.4 us -> 48.6 us
  local copies, waits for them, and re-layouts: 18.3 us -> 24.3 us
    all_to_all x1 -> x0, blocking collectives: 54.5 us -> none  [per_device(): lax.all_to_all(contact_map, 'col', split_axis=0, concat_axis=1, tiled=True)]
    ppermute x0 -> x3, waiting for transfers between devices: none -> 43.9 us  [rotated_exchange(): lax.ppermute(sent, axis, [(d, (d + far) % ways) for d in range(ways)])]
    unnamed x8 -> x19, local copies, waits for them, and re-layouts: 1.28 us -> 7.56 us
    ppermute x0 -> x3, starting transfers between devices: none -> 6.01 us  [rotated_exchange(): lax.ppermute(sent, axis, [(d, (d + far) % ways) for d in range(ways)])]
  transfers between devices with their start and end apart: 13 -> 16, of which waited for: 7 -> 9; matrix products, arithmetic and copies ran while one was open for 13% -> 13% of each run, Pallas kernels for 0% -> 0%
where the time goes in v1:
time: 514 us; the launch traced here: 508 us
  matrix products  200 us (39%)
  blocking collectives  116 us (23%)
  waiting for transfers between devices  115 us (22%)
  starting transfers between devices  48.6 us (9%)
  local copies, waits for them, and re-layouts  24.3 us (5%)
    dot_general x54, matrix products, convolve(): jnp.dot(piece, kernel[tap_row, tap_col], preferred_element_type=jnp.float32)  200 us
    all_to_all x1, blocking collectives, per_device(): lax.all_to_all(current, ('row', 'col'), split_axis=1, concat_axis=0, tile...  59.4 us
    all_to_all x1, blocking collectives, per_device(): lax.all_to_all(current, 'col', split_axis=1, concat_axis=0, tiled=True)  56.1 us
    all_to_all x1, waiting for transfers between devices, per_device(): lax.all_to_all(current, ('row', 'col'), split_axis=1, concat_axis=0, tile...  44.6 us
    ppermute x3, waiting for transfers between devices, rotated_exchange(): lax.ppermute(sent, axis, [(d, (d + far) % ways) for d in range(ways)])  43.9 us
    ppermute x6, starting transfers between devices, with_halo(): before = lax.ppermute(last, axis, up)  29.4 us
    ppermute x6, waiting for transfers between devices, with_halo(): after = lax.ppermute(initial, axis, down)  23.5 us
  transfers between devices with their start and end apart: 16, of which 9 were waited for; matrix products, arithmetic and copies ran while one was open for 13% of the time, Pallas kernels for 0%

profile of v1, /device:TPU:0, one launch (start us, length us, event | category | flops | bytes accessed | tf_op | source)
XLA Modules:
  0.0 508.4 jit_solution(198065559067813222)
XLA Ops:
  3.6 5.0 collective-permute-start
  9.6 11.7 %collective-permute-done = bf16[16,128,128]{2,1,0:T(8,128)(2,1)S(1)} collective-permute-done((bf16[16,128,128]{2,1,0:T(8,128)(2,1)}, bf16[16,128,128]{2,1,0:T(8,128)(2,1)S(1)}, u32[]{:S(2)}, u32[]{:S(2)}) %collective-permute-start) | collective-permute-done | bytes 524320 | tf_op jit(solution)/shard_map/ppermute | solution.py:14
  21.3 32.2 %collective-permute-done.1 = bf16[16,128,128]{2,1,0:T(8,128)(2,1)S(1)} collective-permute-done((bf16[16,128,128]{2,1,0:T(8,128)(2,1)}, bf16[16,128,128]{2,1,0:T(8,128)(2,1)S(1)}, u32[]{:S(2)}, u32[]{:S(2)}) %collective-permute-start.1) | collective-permute-done | bytes 524320 | tf_op jit(solution)/shard_map/ppermute | solution.py:14
  61.0 5.1 %all-to-all-start = ((bf16[16,512,128]{2,0,1:T(8,128)(2,1)}), bf16[16,512,128]{2,0,1:T(8,128)(2,1)S(1)}, u32[]{:S(2)}, u32[]{:S(2)}) async-start(bf16[16,512,128]{2,0,1:T(8,128)(2,1)} %copy.7), calls=%async_computation | async-start | bytes 4194304 | tf_op jit(solution)/shard_map/all_to_all | solution.py:77
  69.1 44.6 %all-to-all-done = bf16[16,512,128]{2,0,1:T(8,128)(2,1)S(1)} async-done(((bf16[16,512,128]{2,0,1:T(8,128)(2,1)}), bf16[16,512,128]{2,0,1:T(8,128)(2,1)S(1)}, u32[]{:S(2)}, u32[]{:S(2)}) %all-to-all-start) | async-done | bytes 2097184 | tf_op jit(solution)/shard_map/all_to_all | solution.py:77
  126.8 6.2 %collective-permute-start.3 = (bf16[1,514,128]{2,1,0:T(8,128)(2,1)S(1)}, bf16[1,514,128]{2,1,0:T(8,128)(2,1)S(1)}, u32[]{:S(2)}, u32[]{:S(2)}) collective-permute-start(bf16[1,514,128]{2,1,0:T(8,128)(2,1)S(1)} %get-tuple-element.7), channel_id=1, source_target_pairs={{0,1},{1,2},{2,3},{3,4},{4,5},{5,6},{6,7},{7,8},{8,9},{9,10},{10,1... | collective-permute-start | bytes 394760 | tf_op jit(solution)/shard_map/ppermute | solution.py:26
  144.2 2.7 fusion.105
  147.0 11.9 %maximum_convert_fusion.3 = bf16[16,512,128]{2,1,0:T(8,128)(2,1)S(1)} fusion(f32[16,512,128]{2,1,0:T(8,128)} %fusion.65, f32[16,512,128]{2,1,0:T(8,128)} %fusion.68, f32[16,512,128]{2,1,0:T(8,128)} %fusion.129, f32[16,512,128]{2,1,0:T(8,128)} %fusion.146, f32[16,512,128]{2,1,0:T(8,128)} %fusion.131, f32[16,512,128]{2,1,0:T(8,128)} %fusion.105, ...), kind=kOutput, calls=%fused_computation.13 | convolution fusion | flops 284164096 | bytes 37947904 | tf_op jit(solution)/shard_map/dot_general | solution.py:40
  165.3 3.9 collective-permute-start.5
  173.4 10.3 %collective-permute-done.6 = bf16[2,516,128]{2,1,0:T(8,128)(2,1)S(1)} collective-permute-done((bf16[2,516,128]{2,1,0:T(8,128)(2,1)S(1)}, bf16[2,516,128]{2,1,0:T(8,128)(2,1)S(1)}, u32[]{:S(2)}, u32[]{:S(2)}) %collective-permute-start.6) | collective-permute-done | bytes 264224 | tf_op jit(solution)/shard_map/ppermute | solution.py:27
  186.4 2.7 fusion.20
  197.2 11.9 %maximum_convert_fusion.2 = bf16[16,512,128]{2,1,0:T(8,128)(2,1)S(1)} fusion(f32[16,512,128]{2,1,0:T(8,128)} %fusion.17, f32[16,512,128]{2,1,0:T(8,128)} %fusion.20, f32[16,512,128]{2,1,0:T(8,128)} %fusion.125, f32[16,512,128]{2,1,0:T(8,128)} %fusion.145, f32[16,512,128]{2,1,0:T(8,128)} %fusion.127, f32[16,512,128]{2,1,0:T(8,128)} %fusion.99, ...), kind=kOutput, calls=%fused_computation.12 | convolution fusion | flops 284164096 | bytes 38081024 | tf_op jit(solution)/shard_map/dot_general | solution.py:40
  216.7 4.8 collective-permute-start.7
  240.5 11.8 %add_convert_fusion.1 = bf16[16,512,128]{2,1,0:T(8,128)(2,1)S(1)} fusion(f32[16,512,128]{2,1,0:T(8,128)} %fusion.41, f32[16,512,128]{2,1,0:T(8,128)} %fusion.44, f32[16,512,128]{2,1,0:T(8,128)} %fusion.121, f32[16,512,128]{2,1,0:T(8,128)} %fusion.144, f32[16,512,128]{2,1,0:T(8,128)} %fusion.123, f32[16,512,128]{2,1,0:T(8,128)} %fusion.95, ...), kind=kOutput, calls=%fused_computation.11 | convolution fusion | flops 285212672 | bytes 40444416 | tf_op jit(solution)/shard_map/dot_general | solution.py:40
  253.6 59.4 %all_to_all.36 = bf16[16,512,128]{2,0,1:T(8,128)(2,1)S(1)} all-to-all(bf16[16,512,128]{2,0,1:T(8,128)(2,1)S(1)} %copy.9), channel_id=1, replica_groups=mesh['row'=8,'col'=4] {'row','col'}, dimensions={1} | all-to-all | bytes 4194304 | tf_op jit(solution)/shard_map/all_to_all | solution.py:77
  324.0 6.0 %collective-permute-start.9 = (bf16[1,514,128]{2,1,0:T(8,128)(2,1)S(1)}, bf16[1,514,128]{2,1,0:T(8,128)(2,1)S(1)}, u32[]{:S(2)}, u32[]{:S(2)}) collective-permute-start(bf16[1,514,128]{2,1,0:T(8,128)(2,1)S(1)} %get-tuple-element.5), channel_id=1, source_target_pairs={{0,1},{1,2},{2,3},{3,4},{4,5},{5,6},{6,7},{7,8},{8,9},{9,10},{10,1... | collective-permute-start | bytes 394760 | tf_op jit(solution)/shard_map/ppermute | solution.py:26
  343.6 11.9 %maximum_convert_fusion.1 = bf16[16,512,128]{2,1,0:T(8,128)(2,1)S(1)} fusion(f32[16,512,128]{2,1,0:T(8,128)} %fusion.53, f32[16,512,128]{2,1,0:T(8,128)} %fusion.56, f32[16,512,128]{2,1,0:T(8,128)} %fusion.117, f32[16,512,128]{2,1,0:T(8,128)} %fusion.143, f32[16,512,128]{2,1,0:T(8,128)} %fusion.119, f32[16,512,128]{2,1,0:T(8,128)} %fusion.89, ...), kind=kOutput, calls=%fused_computation.10 | convolution fusion | flops 284164096 | bytes 37947904 | tf_op jit(solution)/shard_map/dot_general | solution.py:40
  361.6 3.9 collective-permute-start.11
  369.5 11.2 %collective-permute-done.12 = bf16[2,516,128]{2,1,0:T(8,128)(2,1)S(1)} collective-permute-done((bf16[2,516,128]{2,1,0:T(8,128)(2,1)S(1)}, bf16[2,516,128]{2,1,0:T(8,128)(2,1)S(1)}, u32[]{:S(2)}, u32[]{:S(2)}) %collective-permute-start.12) | collective-permute-done | bytes 264224 | tf_op jit(solution)/shard_map/ppermute | solution.py:27
  391.4 2.7 fusion.83
  394.1 11.9 %maximum_convert_fusion = bf16[16,512,128]{2,1,0:T(8,128)(2,1)S(1)} fusion(f32[16,512,128]{2,1,0:T(8,128)} %fusion.5, f32[16,512,128]{2,1,0:T(8,128)} %fusion.8, f32[16,512,128]{2,1,0:T(8,128)} %fusion.113, f32[16,512,128]{2,1,0:T(8,128)} %fusion.142, f32[16,512,128]{2,1,0:T(8,128)} %fusion.115, f32[16,512,128]{2,1,0:T(8,128)} %fusion.83, ...), kind=kOutput, calls=%fused_computation.9 | convolution fusion | flops 284164096 | bytes 38081024 | tf_op jit(solution)/shard_map/dot_general | solution.py:40
  413.8 4.6 collective-permute-start.13
  437.1 11.8 %add_convert_fusion = bf16[16,512,128]{2,1,0:T(8,128)(2,1)S(1)} fusion(f32[16,512,128]{2,1,0:T(8,128)} %fusion.29, f32[16,512,128]{2,1,0:T(8,128)} %fusion.32, f32[16,512,128]{2,1,0:T(8,128)} %fusion.109, f32[16,512,128]{2,1,0:T(8,128)} %fusion.141, f32[16,512,128]{2,1,0:T(8,128)} %fusion.111, f32[16,512,128]{2,1,0:T(8,128)} %fusion.79, ...), kind=kOutput, calls=%fused_computation.8 | convolution fusion | flops 285212672 | bytes 40444416 | tf_op jit(solution)/shard_map/dot_general | solution.py:40
  450.2 56.1 %all_to_all.37 = bf16[16,512,128]{2,0,1:T(8,128)(2,1)S(1)} all-to-all(bf16[16,512,128]{2,0,1:T(8,128)(2,1)S(1)} %copy.11), channel_id=1, replica_groups=mesh['row'=8,'col'=4] {'col'}, dimensions={1} | all-to-all | bytes 4194304 | tf_op jit(solution)/shard_map/all_to_all | solution.py:80
  (109 shorter events, 163.4 us)
Async XLA Ops:
  3.6 17.7 %collective-permute-start = (bf16[16,128,128]{2,1,0:T(8,128)(2,1)}, bf16[16,128,128]{2,1,0:T(8,128)(2,1)S(1)}, u32[]{:S(2)}, u32[]{:S(2)}) collective-permute-start(bf16[16,128,128]{2,1,0:T(8,128)(2,1)} %get-tuple-element.19), channel_id=1, source_target_pairs={{0,3},{1,0},{2,1},{3,2},{4,7},{5,4},{6,5},{7,6},{8,11},{9,8},{10,9... | collective-permute-start | bytes 1572872 | tf_op jit(solution)/shard_map/ppermute | solution.py:14
  8.6 44.9 %collective-permute-start.1 = (bf16[16,128,128]{2,1,0:T(8,128)(2,1)}, bf16[16,128,128]{2,1,0:T(8,128)(2,1)S(1)}, u32[]{:S(2)}, u32[]{:S(2)}) collective-permute-start(bf16[16,128,128]{2,1,0:T(8,128)(2,1)} %get-tuple-element.18), channel_id=1, source_target_pairs={{0,2},{1,3},{2,0},{3,1},{4,6},{5,7},{6,4},{7,5},{8,10},{9,11},{10,... | collective-permute-start | bytes 1572872 | tf_op jit(solution)/shard_map/ppermute | solution.py:14
  8.6 45.0 %collective-permute-start.2 = (bf16[16,128,128]{2,1,0:T(8,128)(2,1)}, bf16[16,128,128]{2,1,0:T(8,128)(2,1)}, u32[]{:S(2)}, u32[]{:S(2)}) collective-permute-start(bf16[16,128,128]{2,1,0:T(8,128)(2,1)} %get-tuple-element.17), channel_id=1, source_target_pairs={{0,1},{1,2},{2,3},{3,0},{4,5},{5,6},{6,7},{7,4},{8,9},{9,10},{10,1... | collective-permute-start | bytes 1572872 | tf_op jit(solution)/shard_map/ppermute | solution.py:14
  56.2 2.0 copy-start
  61.0 5.1 %copy-start.4 = (f32[2,3,128]{2,0,1:T(2,128)S(1)}, f32[2,3,128]{2,0,1:T(2,128)}, u32[]{:S(2)}) copy-start(f32[2,3,128]{2,0,1:T(2,128)} %param.5) | copy-start | bytes 9220
  61.0 52.6 %all-to-all-start = ((bf16[16,512,128]{2,0,1:T(8,128)(2,1)}), bf16[16,512,128]{2,0,1:T(8,128)(2,1)S(1)}, u32[]{:S(2)}, u32[]{:S(2)}) async-start(bf16[16,512,128]{2,0,1:T(8,128)(2,1)} %copy.7), calls=%async_computation | async-start | bytes 4194304 | tf_op jit(solution)/shard_map/all_to_all | solution.py:77
  113.7 2.2 copy-start.1
  116.5 1.0 copy-start.3
  122.8 10.7 %collective-permute-start.4 = (bf16[1,514,128]{2,1,0:T(8,128)(2,1)S(1)}, bf16[1,514,128]{2,1,0:T(8,128)(2,1)S(1)}, u32[]{:S(2)}, u32[]{:S(2)}) collective-permute-start(bf16[1,514,128]{2,1,0:T(8,128)(2,1)S(1)} %get-tuple-element.8), channel_id=1, source_target_pairs={{1,0},{2,1},{3,2},{4,3},{5,4},{6,5},{7,6},{8,7},{9,8},{10,9},{11,1... | collective-permute-start | bytes 394760 | tf_op jit(solution)/shard_map/ppermute | solution.py:27
  126.8 12.1 %collective-permute-start.3 = (bf16[1,514,128]{2,1,0:T(8,128)(2,1)S(1)}, bf16[1,514,128]{2,1,0:T(8,128)(2,1)S(1)}, u32[]{:S(2)}, u32[]{:S(2)}) collective-permute-start(bf16[1,514,128]{2,1,0:T(8,128)(2,1)S(1)} %get-tuple-element.7), channel_id=1, source_target_pairs={{0,1},{1,2},{2,3},{3,4},{4,5},{5,6},{6,7},{7,8},{8,9},{9,10},{10,1... | collective-permute-start | bytes 394760 | tf_op jit(solution)/shard_map/ppermute | solution.py:26
  159.1 1.0 copy-start.2
  165.3 23.8 %collective-permute-start.5 = (bf16[2,516,128]{2,1,0:T(8,128)(2,1)S(1)}, bf16[2,516,128]{2,1,0:T(8,128)(2,1)S(1)}, u32[]{:S(2)}, u32[]{:S(2)}) collective-permute-start(bf16[2,516,128]{2,1,0:T(8,128)(2,1)S(1)} %get-tuple-element.15), channel_id=1, source_target_pairs={{0,1},{1,2},{2,3},{3,4},{4,5},{5,6},{6,7},{7,8},{8,9},{9,10},{10,1... | collective-permute-start | bytes 792584 | tf_op jit(solution)/shard_map/ppermute | solution.py:26
  169.3 14.4 %collective-permute-start.6 = (bf16[2,516,128]{2,1,0:T(8,128)(2,1)S(1)}, bf16[2,516,128]{2,1,0:T(8,128)(2,1)S(1)}, u32[]{:S(2)}, u32[]{:S(2)}) collective-permute-start(bf16[2,516,128]{2,1,0:T(8,128)(2,1)S(1)} %get-tuple-element.16), channel_id=1, source_target_pairs={{1,0},{2,1},{3,2},{4,3},{5,4},{6,5},{7,6},{8,7},{9,8},{10,9},{11,1... | collective-permute-start | bytes 792584 | tf_op jit(solution)/shard_map/ppermute | solution.py:27
  209.4 15.9 %collective-permute-start.8 = (bf16[4,520,128]{2,1,0:T(8,128)(2,1)S(1)}, bf16[4,520,128]{2,1,0:T(8,128)(2,1)S(1)}, u32[]{:S(2)}, u32[]{:S(2)}) collective-permute-start(bf16[4,520,128]{2,1,0:T(8,128)(2,1)S(1)} %get-tuple-element.14), channel_id=1, source_target_pairs={{1,0},{2,1},{3,2},{4,3},{5,4},{6,5},{7,6},{8,7},{9,8},{10,9},{11,1... | collective-permute-start | bytes 1597448 | tf_op jit(solution)/shard_map/ppermute | solution.py:27
  216.7 15.7 %collective-permute-start.7 = (bf16[4,520,128]{2,1,0:T(8,128)(2,1)S(1)}, bf16[4,520,128]{2,1,0:T(8,128)(2,1)S(1)}, u32[]{:S(2)}, u32[]{:S(2)}) collective-permute-start(bf16[4,520,128]{2,1,0:T(8,128)(2,1)S(1)} %get-tuple-element.13), channel_id=1, source_target_pairs={{0,1},{1,2},{2,3},{3,4},{4,5},{5,6},{6,7},{7,8},{8,9},{9,10},{10,1... | collective-permute-start | bytes 1597448 | tf_op jit(solution)/shard_map/ppermute | solution.py:26
  319.5 10.6 %collective-permute-start.10 = (bf16[1,514,128]{2,1,0:T(8,128)(2,1)S(1)}, bf16[1,514,128]{2,1,0:T(8,128)(2,1)S(1)}, u32[]{:S(2)}, u32[]{:S(2)}) collective-permute-start(bf16[1,514,128]{2,1,0:T(8,128)(2,1)S(1)} %get-tuple-element.6), channel_id=1, source_target_pairs={{1,0},{2,1},{3,2},{4,3},{5,4},{6,5},{7,6},{8,7},{9,8},{10,9},{11,1... | collective-permute-start | bytes 394760 | tf_op jit(solution)/shard_map/ppermute | solution.py:27
  324.0 11.5 %collective-permute-start.9 = (bf16[1,514,128]{2,1,0:T(8,128)(2,1)S(1)}, bf16[1,514,128]{2,1,0:T(8,128)(2,1)S(1)}, u32[]{:S(2)}, u32[]{:S(2)}) collective-permute-start(bf16[1,514,128]{2,1,0:T(8,128)(2,1)S(1)} %get-tuple-element.5), channel_id=1, source_target_pairs={{0,1},{1,2},{2,3},{3,4},{4,5},{5,6},{6,7},{7,8},{8,9},{9,10},{10,1... | collective-permute-start | bytes 394760 | tf_op jit(solution)/shard_map/ppermute | solution.py:26
  361.6 24.5 %collective-permute-start.11 = (bf16[2,516,128]{2,1,0:T(8,128)(2,1)S(1)}, bf16[2,516,128]{2,1,0:T(8,128)(2,1)S(1)}, u32[]{:S(2)}, u32[]{:S(2)}) collective-permute-start(bf16[2,516,128]{2,1,0:T(8,128)(2,1)S(1)} %get-tuple-element.11), channel_id=1, source_target_pairs={{0,1},{1,2},{2,3},{3,4},{4,5},{5,6},{6,7},{7,8},{8,9},{9,10},{10,1... | collective-permute-start | bytes 792584 | tf_op jit(solution)/shard_map/ppermute | solution.py:26
  365.5 15.2 %collective-permute-start.12 = (bf16[2,516,128]{2,1,0:T(8,128)(2,1)S(1)}, bf16[2,516,128]{2,1,0:T(8,128)(2,1)S(1)}, u32[]{:S(2)}, u32[]{:S(2)}) collective-permute-start(bf16[2,516,128]{2,1,0:T(8,128)(2,1)S(1)} %get-tuple-element.12), channel_id=1, source_target_pairs={{1,0},{2,1},{3,2},{4,3},{5,4},{6,5},{7,6},{8,7},{9,8},{10,9},{11,1... | collective-permute-start | bytes 792584 | tf_op jit(solution)/shard_map/ppermute | solution.py:27
  406.4 15.5 %collective-permute-start.14 = (bf16[4,520,128]{2,1,0:T(8,128)(2,1)S(1)}, bf16[4,520,128]{2,1,0:T(8,128)(2,1)S(1)}, u32[]{:S(2)}, u32[]{:S(2)}) collective-permute-start(bf16[4,520,128]{2,1,0:T(8,128)(2,1)S(1)} %get-tuple-element.10), channel_id=1, source_target_pairs={{1,0},{2,1},{3,2},{4,3},{5,4},{6,5},{7,6},{8,7},{9,8},{10,9},{11,1... | collective-permute-start | bytes 1597448 | tf_op jit(solution)/shard_map/ppermute | solution.py:27
  413.8 15.2 %collective-permute-start.13 = (bf16[4,520,128]{2,1,0:T(8,128)(2,1)S(1)}, bf16[4,520,128]{2,1,0:T(8,128)(2,1)S(1)}, u32[]{:S(2)}, u32[]{:S(2)}) collective-permute-start(bf16[4,520,128]{2,1,0:T(8,128)(2,1)S(1)} %get-tuple-element.9), channel_id=1, source_target_pairs={{0,1},{1,2},{2,3},{3,4},{4,5},{5,6},{6,7},{7,8},{8,9},{9,10},{10,1... | collective-permute-start | bytes 1597448 | tf_op jit(solution)/shard_map/ppermute | solution.py:26
  434.4 2.7 copy-start.5
